TPU v7x, 32 devices: a whole 2x2x4 slice. The times are simulated.
32 devices in a mesh: fsdp: 4 (over y, x), context: 4 (over z), tensor: 2 (over core).
Axes of the slice: x: 2, y: 2, z: 4, core: 2. Of those that a mesh axis runs over, the one named last changes fastest.
Arguments:
- tokens: bfloat16 [2, 4096, 2048], P(None, ('fsdp', 'context')), may hold values from -6 to 6
- cotangent: bfloat16 [2, 4096, 2048], P(None, ('fsdp', 'context')), may hold values from -6 to 6
- seg_parent: int32 [2, 32], P(None, 'fsdp'), may hold values from -1 to 7, as said below
- positions: int32 [2, 4096], P(None, 'fsdp'), may hold values from 0 to 895, as said below
- norm_gain: bfloat16 [2, 2048], P(None, 'fsdp'), may hold values from 0.5 to 1.5
- norm_bias: bfloat16 [2, 2048], P(None, 'fsdp'), may hold values from -1.1953125 to 1.1953125
- w_qkv: bfloat16 [3, 2048, 2048], P(None, 'fsdp', 'tensor'), may hold values from -0.125 to 0.125
- bias_qv: bfloat16 [2, 2048], P(None, ('tensor', 'fsdp')), may hold values from -1.1953125 to 1.1953125
- w_out: bfloat16 [2048, 2048], P('tensor', 'fsdp'), may hold values from -0.25 to 0.25
- bias_out: bfloat16 [2048], P('fsdp'), may hold values from -1.1953125 to 1.1953125
- w_up: bfloat16 [2048, 8192], P('fsdp', 'tensor'), may hold values from -0.125 to 0.125
- bias_up: bfloat16 [8192], P(('tensor', 'fsdp')), may hold values from -1.1953125 to 1.1953125
- w_down: bfloat16 [8192, 2048], P('tensor', 'fsdp'), may hold values from -0.0625 to 0.0625
- bias_down: bfloat16 [2048], P('fsdp'), may hold values from -1.1953125 to 1.1953125
Outputs:
- layer_out: bfloat16 [2, 4096, 2048], P(None, ('fsdp', 'context'))
- grad_tokens: bfloat16 [2, 4096, 2048], P(None, ('fsdp', 'context'))
- grad_norm_gain: float32 [2, 2048], P(None, 'fsdp')
- grad_norm_bias: float32 [2, 2048], P(None, 'fsdp')
- grad_w_qkv: float32 [3, 2048, 2048], P(None, 'fsdp', 'tensor')
- grad_bias_qv: float32 [2, 2048], P(None, ('tensor', 'fsdp'))
- grad_w_out: float32 [2048, 2048], P('tensor', 'fsdp')
- grad_bias_out: float32 [2048], P('fsdp')
- grad_w_up: float32 [2048, 8192], P('fsdp', 'tensor')
- grad_bias_up: float32 [8192], P(('tensor', 'fsdp'))
- grad_w_down: float32 [8192, 2048], P('tensor', 'fsdp')
- grad_bias_down: float32 [2048], P('fsdp')
Inputs may be any that keep to these rules, and one draw needn't show every extreme that they name: `seg_parent`: each micro-batch holds 4 trees of 8 entries; a tree is a trunk of 5 segments in a chain from a root, 1 branches whose parent is the trunk's last segment, and 2 leaves whose parent is each branch; which slot holds which segment is a permutation drawn from the seed for each tree. `positions`: A token's position is the depth of its segment in its tree times 128 plus its place within the segment.
All inputs are finite; a program needn't handle non-finite values.
Results may differ from a plain program's by a relative error of at most 0.02.
Values may be sent and summed in bfloat16 or wider, within the bound.
No kernel may reach another device: no remote copies, remote signals or barrier semaphores. Data moves between devices by JAX's collectives and lax.ppermute only.
A program may use at most 384 MiB of HBM per device.

v0:
```python
from functools import partial
import jax
import jax.numpy as jnp
from jax import lax
from jax.sharding import PartitionSpec as P

HEADS = 32
HEAD_DIM = 64
SEG = 128
TRUNK_SEGS = 5
MICRO = 2
HIGHEST_DOT = lax.Precision.HIGHEST
NEG_FILL = -1e30


def product(left_op, right_op):
    return jnp.dot(left_op, right_op, preferred_element_type=jnp.float32)


def across_rows(left_op, right_op):
    return lax.dot_general(
        left_op, right_op, (((0,), (0,)), ((), ())), preferred_element_type=jnp.float32
    )


def across_last(left_op, right_op):
    return lax.dot_general(
        left_op, right_op, (((1,), (1,)), ((), ())), preferred_element_type=jnp.float32
    )


def accumulate(previous, term):
    return previous + term


def norm_rows(values_in, gain, shift):
    row_mean = jnp.mean(values_in, axis=-1, keepdims=True)
    centred = values_in - row_mean
    variance = jnp.mean(centred * centred, axis=-1, keepdims=True)
    return centred * lax.rsqrt(variance + 1e-05) * gain + shift


def ancestry_table(parents):
    slot_ids = jnp.arange(parents.shape[0], dtype=jnp.int32)
    parent_step = (parents[:, None] == slot_ids[None, :]).astype(jnp.float32)
    reach_now = jnp.eye(parents.shape[0], dtype=jnp.float32)
    reached = reach_now
    for depth_step in range(TRUNK_SEGS + 1):
        reach_now = jnp.dot(reach_now, parent_step, precision=HIGHEST_DOT)
        reached = reached + reach_now
    return reached > 0.5


def exact_gelu(pre_act):
    return jax.nn.gelu(pre_act, approximate=False)


def head_first(matrix):
    return matrix.reshape(matrix.shape[0], matrix.shape[1] // HEAD_DIM, HEAD_DIM).transpose(1, 0, 2)


def rows_first(stacked):
    return stacked.transpose(1, 0, 2).reshape(stacked.shape[1], stacked.shape[0] * stacked.shape[2])


def masked_scores(queries, key_rows, head_slope, allowed, offsets):
    raw_scores = jnp.einsum("qd,kd->qk", queries, key_rows, preferred_element_type=jnp.float32)
    return jnp.where(allowed, raw_scores * HEAD_DIM ** (-0.5) + head_slope * offsets, NEG_FILL)


def head_forward(packed, allowed, offsets):
    queries, key_rows, values, head_slope = packed
    scores = masked_scores(queries, key_rows, head_slope, allowed, offsets)
    highest = jnp.max(scores, axis=-1, keepdims=True)
    raised = jnp.exp(scores - highest)
    row_total = jnp.sum(raised, axis=-1, keepdims=True)
    probabilities = (raised / row_total).astype(jnp.bfloat16)
    attended = product(probabilities, values)
    return (attended, (highest + jnp.log(row_total))[:, 0], probabilities)


def head_backward(packed, allowed, offsets):
    queries, key_rows, values, grad_out, head_slope, log_total = packed
    scores = masked_scores(queries, key_rows, head_slope, allowed, offsets)
    probabilities = jnp.exp(scores - log_total[:, None])
    grad_probs = jnp.einsum("qd,kd->qk", grad_out, values, preferred_element_type=jnp.float32)
    centre = jnp.sum(probabilities * grad_probs, axis=-1, keepdims=True)
    grad_scores = (probabilities * (grad_probs - centre)).astype(jnp.bfloat16)
    grad_queries = product(grad_scores, key_rows) * HEAD_DIM ** (-0.5)
    return (grad_queries, grad_scores)


def layer_pass(gathered, running, hidden_bf, grad_bf, parents, places, first_slot, slopes):
    norm_gains, norm_shifts, w_qkv, bias_qv, w_out, bias_out, w_up, bias_up, w_down, bias_down = (
        gathered
    )
    local_rows = hidden_bf.shape[0]
    hidden_in = hidden_bf.astype(jnp.float32)
    normed_f, norm_back = jax.vjp(
        norm_rows, hidden_in, norm_gains[0].astype(jnp.float32), norm_shifts[0].astype(jnp.float32)
    )
    normed = normed_f.astype(jnp.bfloat16)
    queries = (product(normed, w_qkv[0]) + bias_qv[0].astype(jnp.float32)).astype(jnp.bfloat16)
    key_rows = product(normed, w_qkv[1]).astype(jnp.bfloat16)
    values = (product(normed, w_qkv[2]) + bias_qv[1].astype(jnp.float32)).astype(jnp.bfloat16)
    all_keys, all_values = (
        lax.all_gather(key_rows, "context", axis=0, tiled=True),
        lax.all_gather(values, "context", axis=0, tiled=True),
    )
    ancestry = ancestry_table(parents)
    own_rows = lax.dynamic_slice_in_dim(ancestry, first_slot, local_rows // SEG, 0)
    allowed_slots = jnp.repeat(jnp.repeat(own_rows, SEG, axis=0), SEG, axis=1)
    query_places = lax.dynamic_slice_in_dim(places, first_slot * SEG, local_rows, 0)
    allowed = allowed_slots & (places[None, :] <= query_places[:, None])
    offsets = (places[None, :] - query_places[:, None]).astype(jnp.float32)
    head_queries = head_first(queries)
    head_keys = head_first(all_keys)
    head_values = head_first(all_values)
    head_out, log_total, kept_probs = lax.map(
        partial(head_forward, allowed=allowed, offsets=offsets),
        (head_queries, head_keys, head_values, slopes),
    )
    attended = rows_first(head_out).astype(jnp.bfloat16)
    branch = lax.psum(product(attended, w_out).astype(jnp.bfloat16), "tensor").astype(
        jnp.float32
    ) + bias_out.astype(jnp.float32)
    middle = hidden_in + branch
    normed_two_f, norm_two_back = jax.vjp(
        norm_rows, middle, norm_gains[1].astype(jnp.float32), norm_shifts[1].astype(jnp.float32)
    )
    normed_two = normed_two_f.astype(jnp.bfloat16)
    pre_act = product(normed_two, w_up) + bias_up.astype(jnp.float32)
    activated_f, gelu_back = jax.vjp(exact_gelu, pre_act)
    activated = activated_f.astype(jnp.bfloat16)
    layer_out = middle + (
        lax.psum(product(activated, w_down).astype(jnp.bfloat16), "tensor").astype(jnp.float32)
        + bias_down.astype(jnp.float32)
    )
    grad_w_down = across_rows(activated, grad_bf)
    grad_bias_down = jnp.sum(grad_bf.astype(jnp.float32), axis=0)
    grad_pre = gelu_back(across_last(grad_bf, w_down))[0].astype(jnp.bfloat16)
    grad_w_up = across_rows(normed_two, grad_pre)
    grad_bias_up = jnp.sum(grad_pre.astype(jnp.float32), axis=0)
    grad_normed_two = lax.psum(across_last(grad_pre, w_up).astype(jnp.bfloat16), "tensor").astype(
        jnp.float32
    )
    grad_middle_norm, grad_gain_two, grad_shift_two = norm_two_back(grad_normed_two)
    grad_middle = grad_bf.astype(jnp.float32) + grad_middle_norm
    grad_branch = grad_middle.astype(jnp.bfloat16)
    grad_w_out = across_rows(attended, grad_branch)
    grad_bias_out = jnp.sum(grad_branch.astype(jnp.float32), axis=0)
    grad_attended = across_last(grad_branch, w_out).astype(jnp.bfloat16)
    head_grads = head_first(grad_attended)
    grad_head_queries, grad_scores = lax.map(
        partial(head_backward, allowed=allowed, offsets=offsets),
        (head_queries, head_keys, head_values, head_grads, slopes, log_total),
    )
    grad_queries = rows_first(grad_head_queries).astype(jnp.bfloat16)
    grad_keys_part = jnp.einsum(
        "hqk,hqd->khd", grad_scores, head_queries, preferred_element_type=jnp.float32
    ) * HEAD_DIM ** (-0.5)
    grad_values_part = jnp.einsum(
        "hqk,hqd->khd", kept_probs, head_grads, preferred_element_type=jnp.float32
    )
    key_grads = lax.psum_scatter(
        jnp.stack(
            [
                grad_keys_part.reshape(local_rows * lax.axis_size("context"), -1),
                grad_values_part.reshape(local_rows * lax.axis_size("context"), -1),
            ],
            axis=1,
        ).astype(jnp.bfloat16),
        "context",
        scatter_dimension=0,
        tiled=True,
    ).astype(jnp.float32)
    grad_keys = key_grads[:, 0].astype(jnp.bfloat16)
    grad_values = key_grads[:, 1].astype(jnp.bfloat16)
    grad_w_qkv = jnp.stack(
        [
            across_rows(normed, grad_queries),
            across_rows(normed, grad_keys),
            across_rows(normed, grad_values),
        ]
    )
    grad_bias_qv = jnp.stack(
        [
            jnp.sum(grad_queries.astype(jnp.float32), axis=0),
            jnp.sum(grad_values.astype(jnp.float32), axis=0),
        ]
    )
    grad_normed = lax.psum(
        (
            across_last(grad_queries, w_qkv[0])
            + across_last(grad_keys, w_qkv[1])
            + across_last(grad_values, w_qkv[2])
        ).astype(jnp.bfloat16),
        "tensor",
    ).astype(jnp.float32)
    grad_input_norm, grad_gain_one, grad_shift_one = norm_back(grad_normed)
    grad_tokens = grad_middle + grad_input_norm
    fresh = (
        jnp.stack([grad_gain_one, grad_gain_two]),
        jnp.stack([grad_shift_one, grad_shift_two]),
        grad_w_qkv,
        grad_bias_qv,
        grad_w_out,
        grad_bias_out,
        grad_w_up,
        grad_bias_up,
        grad_w_down,
        grad_bias_down,
    )
    if running is None:
        summed = fresh
    else:
        summed = tuple((accumulate(previous, term) for previous, term in zip(running, fresh)))
    return (layer_out.astype(jnp.bfloat16), grad_tokens.astype(jnp.bfloat16), summed)


def per_device(
    tokens,
    cotangent,
    seg_parent,
    positions,
    norm_gain,
    norm_bias,
    w_qkv,
    bias_qv,
    w_out,
    bias_out,
    w_up,
    bias_up,
    w_down,
    bias_down,
):
    local_rows = tokens.shape[1]
    first_slot = lax.axis_index("context") * (local_rows // SEG)
    local_heads = w_qkv.shape[2] // HEAD_DIM
    head_ids = lax.axis_index("tensor") * local_heads + jnp.arange(local_heads, dtype=jnp.int32)
    slopes = jnp.exp2(-8.0 * (head_ids + 1).astype(jnp.float32) / HEADS)
    gathered = None
    outputs = []
    input_grads = []
    totals = None
    for batch_index in range(MICRO):
        gathered = (
            lax.all_gather(norm_gain, "fsdp", axis=1, tiled=True),
            lax.all_gather(norm_bias, "fsdp", axis=1, tiled=True),
            lax.all_gather(w_qkv, "fsdp", axis=1, tiled=True),
            lax.all_gather(bias_qv, "fsdp", axis=1, tiled=True),
            lax.all_gather(w_out, "fsdp", axis=1, tiled=True),
            lax.all_gather(bias_out, "fsdp", axis=0, tiled=True),
            lax.all_gather(w_up, "fsdp", axis=0, tiled=True),
            lax.all_gather(bias_up, "fsdp", axis=0, tiled=True),
            lax.all_gather(w_down, "fsdp", axis=1, tiled=True),
            lax.all_gather(bias_down, "fsdp", axis=0, tiled=True),
        )
        out_rows, grad_rows, totals = layer_pass(
            gathered,
            totals,
            tokens[batch_index],
            cotangent[batch_index],
            seg_parent[batch_index],
            positions[batch_index],
            first_slot,
            slopes,
        )
        outputs.append(out_rows)
        input_grads.append(grad_rows)
    shard_sums = (
        lax.psum_scatter(
            totals[0].astype(jnp.bfloat16), "fsdp", scatter_dimension=1, tiled=True
        ).astype(jnp.float32),
        lax.psum_scatter(
            totals[1].astype(jnp.bfloat16), "fsdp", scatter_dimension=1, tiled=True
        ).astype(jnp.float32),
        lax.psum_scatter(
            totals[2].astype(jnp.bfloat16), "fsdp", scatter_dimension=1, tiled=True
        ).astype(jnp.float32),
        lax.psum_scatter(
            totals[3].astype(jnp.bfloat16), "fsdp", scatter_dimension=1, tiled=True
        ).astype(jnp.float32),
        lax.psum_scatter(
            totals[4].astype(jnp.bfloat16), "fsdp", scatter_dimension=1, tiled=True
        ).astype(jnp.float32),
        lax.psum_scatter(
            totals[5].astype(jnp.bfloat16), "fsdp", scatter_dimension=0, tiled=True
        ).astype(jnp.float32),
        lax.psum_scatter(
            totals[6].astype(jnp.bfloat16), "fsdp", scatter_dimension=0, tiled=True
        ).astype(jnp.float32),
        lax.psum_scatter(
            totals[7].astype(jnp.bfloat16), "fsdp", scatter_dimension=0, tiled=True
        ).astype(jnp.float32),
        lax.psum_scatter(
            totals[8].astype(jnp.bfloat16), "fsdp", scatter_dimension=1, tiled=True
        ).astype(jnp.float32),
        lax.psum_scatter(
            totals[9].astype(jnp.bfloat16), "fsdp", scatter_dimension=0, tiled=True
        ).astype(jnp.float32),
    )
    reduced = (
        lax.psum(shard_sums[0].astype(jnp.bfloat16), "context").astype(jnp.float32),
        lax.psum(shard_sums[1].astype(jnp.bfloat16), "context").astype(jnp.float32),
        lax.psum(shard_sums[2].astype(jnp.bfloat16), "context").astype(jnp.float32),
        lax.psum(shard_sums[3].astype(jnp.bfloat16), "context").astype(jnp.float32),
        lax.psum(shard_sums[4].astype(jnp.bfloat16), "context").astype(jnp.float32),
        lax.psum(shard_sums[5].astype(jnp.bfloat16), "context").astype(jnp.float32),
        lax.psum(shard_sums[6].astype(jnp.bfloat16), "context").astype(jnp.float32),
        lax.psum(shard_sums[7].astype(jnp.bfloat16), "context").astype(jnp.float32),
        lax.psum(shard_sums[8].astype(jnp.bfloat16), "context").astype(jnp.float32),
        lax.psum(shard_sums[9].astype(jnp.bfloat16), "context").astype(jnp.float32),
    )
    return (
        jnp.stack(outputs),
        jnp.stack(input_grads),
        reduced[0],
        reduced[1],
        reduced[2],
        reduced[3],
        reduced[4],
        reduced[5],
        reduced[6],
        reduced[7],
        reduced[8],
        reduced[9],
    )


def solution(mesh):
    in_specs = (
        P(None, ("fsdp", "context"), None),
        P(None, ("fsdp", "context"), None),
        P(None, "fsdp"),
        P(None, "fsdp"),
        P(None, "fsdp"),
        P(None, "fsdp"),
        P(None, "fsdp", "tensor"),
        P(None, ("tensor", "fsdp")),
        P("tensor", "fsdp"),
        P("fsdp"),
        P("fsdp", "tensor"),
        P(("tensor", "fsdp")),
        P("tensor", "fsdp"),
        P("fsdp"),
    )
    out_specs = (
        P(None, ("fsdp", "context"), None),
        P(None, ("fsdp", "context"), None),
        P(None, "fsdp"),
        P(None, "fsdp"),
        P(None, "fsdp", "tensor"),
        P(None, ("tensor", "fsdp")),
        P("tensor", "fsdp"),
        P("fsdp"),
        P("fsdp", "tensor"),
        P(("tensor", "fsdp")),
        P("tensor", "fsdp"),
        P("fsdp"),
    )
    return jax.shard_map(
        per_device, mesh=mesh, in_specs=in_specs, out_specs=out_specs, check_vma=False
    )
```

profile of v0, /device:TPU:0, one launch (start us, length us, event | category | flops | bytes accessed | tf_op | source)
XLA Modules:
  0.0 2462.3 jit_solution(751354175220968647)
XLA Ops:
  8.0 9.6 all_gather.53
  17.6 7.9 all_gather.52
  26.4 108.7 %all-gather.11.cloned.1.call-done = bf16[3,2048,1024]{2,1,0:T(8,128)(2,1)} async-done(((bf16[3,512,1024]{2,1,0:T(8,128)(2,1)}), bf16[3,2048,1024]{2,1,0:T(8,128)(2,1)}) %all-gather.11.cloned.1.call-update) | async-done | bytes 12582928 | tf_op jit(solution)/shard_map/all_gather | solution.py:250
  139.5 8.0 all_gather.55
  160.1 25.4 %all-gather.13.cloned.1.call-done = bf16[1024,1024]{1,0:T(8,128)(2,1)} async-done(((bf16[256,1024]{1,0:T(8,128)(2,1)}), bf16[1024,1024]{1,0:T(8,128)(2,1)}) %all-gather.13.cloned.1.call-update) | async-done | bytes 2097168 | tf_op jit(solution)/shard_map/all_gather | solution.py:107
  194.3 38.1 %all-gather.15.cloned.1.call-done = bf16[1024,1024]{1,0:T(8,128)(2,1)} async-done(((bf16[256,1024]{1,0:T(8,128)(2,1)}), bf16[1024,1024]{1,0:T(8,128)(2,1)}) %all-gather.15.cloned.1.call-update) | async-done | bytes 2097168 | tf_op jit(solution)/shard_map/all_gather | solution.py:108
  236.3 4.9 copy.65
  246.6 104.7 %while.60 = (s32[]{:T(128)}, bf16[16,256,64]{1,2,0:T(8,128)(2,1)}, f32[16,256]{1,0:T(8,128)S(1)}, bf16[16,256,1024]{2,1,0:T(8,128)(2,1)}, bf16[16,256,64]{2,1,0:...) while((s32[]{:T(128)}, bf16[16,256,64]{1,2,0:T(8,128)(2,1)}, ...), condition=%wide.region_5.6_spmd.clone.clone, body=%wide.region_2.5_spmd.clone.clone.sunk | while | flops 71565056 | bytes 5920409 | solution.py:119
  356.0 8.2 all-gather
  364.2 10.1 all-reduce.14.cloned.1.call-done
  390.1 37.8 %all-gather.23.cloned.1.call-done = bf16[1024,1024]{1,0:T(8,128)(2,1)} async-done(((bf16[256,1024]{1,0:T(8,128)(2,1)}), bf16[1024,1024]{1,0:T(8,128)(2,1)}) %all-gather.23.cloned.1.call-update) | async-done | bytes 2097168 | tf_op jit(solution)/shard_map/all_gather | solution.py:107
  436.7 38.1 %all-gather.25.cloned.1.call-done = bf16[1024,1024]{1,0:T(8,128)(2,1)} async-done(((bf16[256,1024]{1,0:T(8,128)(2,1)}), bf16[1024,1024]{1,0:T(8,128)(2,1)}) %all-gather.25.cloned.1.call-update) | async-done | bytes 2097168 | tf_op jit(solution)/shard_map/all_gather | solution.py:108
  488.9 104.7 %while.61 = (s32[]{:T(128)}, bf16[16,256,64]{1,2,0:T(8,128)(2,1)}, f32[16,256]{1,0:T(8,128)S(1)}, bf16[16,256,1024]{2,1,0:T(8,128)(2,1)}, bf16[16,256,64]{2,1,0:...) while((s32[]{:T(128)}, bf16[16,256,64]{1,2,0:T(8,128)(2,1)}, ...), condition=%wide.region_15.16_spmd.clone.clone, body=%wide.region_12.15_spmd.clone.clone.sunk | while | flops 71565056 | bytes 5920409 | solution.py:119
  599.7 8.2 all_gather.61
  608.0 8.8 all-reduce.16.cloned.1.call-done
  619.6 157.6 %all-gather.19.cloned.1.call-done = bf16[2048,4096]{1,0:T(8,128)(2,1)} async-done(((bf16[512,4096]{1,0:T(8,128)(2,1)}), bf16[2048,4096]{1,0:T(8,128)(2,1)}) %all-gather.19.cloned.1.call-update) | async-done | bytes 16777232 | tf_op jit(solution)/shard_map/all_gather | solution.py:254
  777.2 13.2 convolution_add_fusion
  791.6 6.3 convolution_add_fusion.1
  797.9 138.3 %all-gather.21.cloned.1.call-done = bf16[4096,2048]{1,0:T(8,128)(2,1)} async-done(((bf16[4096,512]{1,0:T(8,128)(2,1)}), bf16[4096,2048]{1,0:T(8,128)(2,1)}) %all-gather.21.cloned.1.call-update) | async-done | bytes 16777232 | tf_op jit(solution)/shard_map/all_gather | solution.py:256
  936.2 20.2 convert_reduce_fusion.1
  956.4 11.9 convolution_convert_fusion.1
  968.3 19.9 convert_reduce_fusion
  988.2 11.9 convolution_convert_fusion
  1000.2 21.4 all-reduce.22.cloned.1.call-done
  1040.1 121.1 %while.62 = (s32[]{:T(128)}, bf16[16,256,64]{1,2,0:T(8,128)(2,1)S(1)}, bf16[16,256,1024]{2,1,0:T(8,128)(2,1)}, bf16[16,256,64]{2,1,0:T(8,128)(2,1)}, bf16[16,102...) while((s32[]{:T(128)}, ...), condition=%wide.region_25.26_spmd.clone.clone, body=%wide.region_23.25_spmd.clone.clone.sunk | while | flops 104349440 | bytes 8306329 | solution.py:154
  1161.3 5.2 convolution_convert_fusion.7
  1180.9 121.3 %while.63 = (s32[]{:T(128)}, bf16[16,256,64]{1,2,0:T(8,128)(2,1)S(1)}, bf16[16,256,1024]{2,1,0:T(8,128)(2,1)}, bf16[16,256,64]{2,1,0:T(8,128)(2,1)}, bf16[16,102...) while((s32[]{:T(128)}, ...), condition=%wide.region_35.36_spmd.clone.clone, body=%wide.region_33.35_spmd.clone.clone.sunk | while | flops 104349440 | bytes 8306329 | solution.py:154
  1302.1 5.2 convolution_convert_fusion.6
  1312.2 17.7 convolution_convert_fusion.2
  1329.9 17.1 convolution_convert_fusion.3
  1361.3 28.9 %reduce-scatter.18.cloned.1.call-done = bf16[256,2,1024]{0,2,1:T(8,128)(2,1)} async-done(((bf16[1024,2,1024]{0,2,1:T(8,128)(2,1)}), bf16[256,2,1024]{0,2,1:T(8,128)(2,1)}) %reduce-scatter.18.cloned.1.call-update) | async-done | bytes 1048592 | tf_op jit(solution)/shard_map/reduce_scatter | solution.py:165
  1409.7 17.0 fusion.233
  1426.7 19.4 add_convert_fusion.1
  1446.3 21.1 fusion.176
  1467.3 25.7 %add_convert_fusion = bf16[4096,2048]{1,0:T(8,128)(2,1)} fusion(f32[4096,2048]{1,0:T(8,128)} %fusion.176, bf16[2,256,2048]{2,1,0:T(8,128)(2,1)} %param.23, f32[256,4096]{1,0:T(8,128)} %convolution_add_fusion), kind=kOutput, calls=%fused_computation.104 | convolution fusion | flops 4379901952 | bytes 55574528 | tf_op jit(solution)/shard_map/dot_general | solution.py:21
  1498.5 4.8 convolution_bitcast_fusion.6
  1503.4 4.8 convolution_bitcast_fusion.2
  1512.9 15.5 fusion.80
  1540.2 102.7 %reduce-scatter.24.cloned.1.call-done = bf16[512,4096]{1,0:T(8,128)(2,1)} async-done(((bf16[2048,4096]{1,0:T(8,128)(2,1)}), bf16[512,4096]{1,0:T(8,128)(2,1)}) %reduce-scatter.24.cloned.1.call-update) | async-done | bytes 4194320 | tf_op jit(solution)/shard_map/reduce_scatter | solution.py:290
  1642.9 157.0 %reduce-scatter.26.cloned.1.call-done = bf16[4096,512]{1,0:T(8,128)(2,1)} async-done(((bf16[4096,2048]{1,0:T(8,128)(2,1)}), bf16[4096,512]{1,0:T(8,128)(2,1)}) %reduce-scatter.26.cloned.1.call-update) | async-done | bytes 4194320 | tf_op jit(solution)/shard_map/reduce_scatter | solution.py:296
  1799.9 124.0 %reduce-scatter.20.cloned.1.call-done = bf16[3,512,1024]{2,1,0:T(8,128)(2,1)} async-done(((bf16[3,2048,1024]{2,1,0:T(8,128)(2,1)}), bf16[3,512,1024]{2,1,0:T(8,128)(2,1)}) %reduce-scatter.20.cloned.1.call-update) | async-done | bytes 3145744 | tf_op jit(solution)/shard_map/reduce_scatter | solution.py:278
  1924.6 7.9 all-gather.1
  1936.4 15.1 all-reduce.5
  1962.4 17.3 reduce-scatter.28.cloned.1.call-done
  1980.6 27.5 %reduce-scatter.30.cloned.1.call-done = bf16[512,2]{1,0:T(8,128)(2,1)} async-done(((bf16[2048,2]{1,0:T(8,128)(2,1)}), bf16[512,2]{1,0:T(8,128)(2,1)}) %reduce-scatter.30.cloned.1.call-update) | async-done | bytes 2064
  2009.1 12.3 all-reduce.3
  2024.9 414.2 %all-reduce.18.cloned.1.call-done = (bf16[3,512,1024]{2,1,0:T(8,128)(2,1)}, bf16[1024,512]{1,0:T(8,128)(2,1)}, bf16[512,4096]{1,0:T(8,128)(2,1)}, bf16[4096,512]{1,0:T(8,128)(2,1)}) async-done(((bf16[3,512,1024]{2,1,0:T(8,128)(2,1)}, bf16[1024,512]{1,0:T(8,128)(2,1)}, bf16[512,4096]{1,0:T(8,128)(2,1)}, bf16[4096,512]{1,0:T(8,128)(2,1)}), (bf16[3,512,1024]{2,1,0:T(8,128)(2,1)}, bf16[1024,512]{1,0:T(8,128)(2,1)}, ...) | async-done | bytes 12582928 | tf_op jit(solution)/shard_map/psum | solution.py:306
  2439.1 5.5 convert_element_type.469
  (895 shorter events, 662.8 us)
Async XLA Ops:
  7.2 127.9 %all-gather.11.cloned.1.call-start = ((), (), s32[]{:S(2)}) async-start(), calls=%async_computation.9 | async-start | bytes 15728640 | tf_op jit(solution)/shard_map/all_gather | solution.py:250
  7.9 177.6 %all-gather.13.cloned.1.call-start = ((), (), s32[]{:S(2)}) async-start(), calls=%async_computation.10 | async-start | bytes 2621440 | tf_op jit(solution)/shard_map/all_gather | solution.py:107
  25.9 129.2 %copy-start.54 = (f32[256]{0:T(256)}, f32[256]{0:T(256)S(1)}, u32[]{:S(2)}) copy-start(f32[256]{0:T(256)S(1)} %broadcast_multiply_fusion.3) | copy-start | bytes 3076
  26.3 113.1 %copy-start.90 = (f32[256]{0:T(256)}, f32[256]{0:T(256)S(1)}, u32[]{:S(2)}) copy-start(f32[256]{0:T(256)S(1)} %fusion.133) | copy-start | bytes 3076
  26.3 128.7 %copy-start.59 = (f32[256]{0:T(256)}, f32[256]{0:T(256)S(1)}, u32[]{:S(2)}) copy-start(f32[256]{0:T(256)S(1)} %fusion.229) | copy-start | bytes 3076
  26.4 358.7 %copy-start.42 = (f32[1,2048]{1,0:T(1,128)}, f32[1,2048]{1,0:T(1,128)S(1)}, u32[]{:S(2)}) copy-start(f32[1,2048]{1,0:T(1,128)S(1)} %get-tuple-element.762) | copy-start | bytes 24580
  26.4 764.1 %copy-start.50 = (f32[1,2048]{1,0:T(1,128)}, f32[1,2048]{1,0:T(1,128)S(1)}, u32[]{:S(2)}) copy-start(f32[1,2048]{1,0:T(1,128)S(1)} %get-tuple-element.761) | copy-start | bytes 24580
  26.4 358.6 %copy-start.27 = (f32[1,2048]{1,0:T(1,128)}, f32[1,2048]{1,0:T(1,128)S(1)}, u32[]{:S(2)}) copy-start(f32[1,2048]{1,0:T(1,128)S(1)} %get-tuple-element.760) | copy-start | bytes 24580
  26.4 1002.6 %copy-start.48 = (f32[1,2048]{1,0:T(1,128)}, f32[1,2048]{1,0:T(1,128)S(1)}, u32[]{:S(2)}) copy-start(f32[1,2048]{1,0:T(1,128)S(1)} %get-tuple-element.759) | copy-start | bytes 24580
  139.4 92.9 %all-gather.15.cloned.1.call-start = ((), (), s32[]{:S(2)}) async-start(), calls=%async_computation.11 | async-start | bytes 2621440 | tf_op jit(solution)/shard_map/all_gather | solution.py:108
  152.0 199.3 %all-gather.17.cloned.1.call-start = ((), (), s32[]{:S(2)}) async-start(), calls=%async_computation.12 | async-start | bytes 5242880 | tf_op jit(solution)/shard_map/all_gather | solution.py:252
  152.6 221.7 %all-reduce.14.cloned.1.call-start = ((), (), s32[]{:S(2)}) async-start(), calls=%async_computation.13 | async-start | bytes 2097152 | tf_op jit(solution)/shard_map/psum | solution.py:124
  158.8 35.4 %copy-start.19 = (bf16[256,1024]{0,1:T(8,128)(2,1)}, bf16[256,1024]{0,1:T(8,128)(2,1)S(1)}, u32[]{:S(2)}) copy-start(bf16[256,1024]{0,1:T(8,128)(2,1)S(1)} %copy.60) | copy-start | bytes 1572868
  351.3 25.0 %copy-start.38 = (pred[256,8]{1,0:T(8,128)(4,1)}, pred[256,8]{1,0:T(8,128)(4,1)S(1)}, u32[]{:S(2)}) copy-start(pred[256,8]{1,0:T(8,128)(4,1)S(1)} %get-tuple-element.1315) | copy-start | bytes 6148
  351.3 25.0 %copy-start.76 = (f32[16,256]{1,0:T(8,128)}, f32[16,256]{1,0:T(8,128)S(1)}, u32[]{:S(2)}) copy-start(f32[16,256]{1,0:T(8,128)S(1)} %get-tuple-element.1163) | copy-start | bytes 49156
  351.3 25.0 %copy-start.95 = (s32[1024]{0:T(1024)}, s32[1024]{0:T(1024)S(1)}, u32[]{:S(2)}) copy-start(s32[1024]{0:T(1024)S(1)} %get-tuple-element.1365) | copy-start | bytes 12292
  351.3 25.0 %copy-start.102 = (s32[256]{0:T(256)}, s32[256]{0:T(256)S(1)}, u32[]{:S(2)}) copy-start(s32[256]{0:T(256)S(1)} %get-tuple-element.1366) | copy-start | bytes 3076
  356.0 72.0 %all-gather.23.cloned.1.call-start = ((), (), s32[]{:S(2)}) async-start(), calls=%async_computation.16 | async-start | bytes 2621440 | tf_op jit(solution)/shard_map/all_gather | solution.py:107
  364.2 664.8 %copy-start.44 = (f32[4,1,512]{2,1,0:T(1,128)}, f32[4,1,512]{2,1,0:T(1,128)S(1)}, u32[]{:S(2)}) copy-start(f32[4,1,512]{2,1,0:T(1,128)S(1)} %convert_element_type.492) | copy-start | bytes 24580
  364.2 20.8 copy-start.52
  380.6 94.2 %all-gather.25.cloned.1.call-start = ((), (), s32[]{:S(2)}) async-start(), calls=%async_computation.17 | async-start | bytes 2621440 | tf_op jit(solution)/shard_map/all_gather | solution.py:108
  385.0 231.8 %all-reduce.16.cloned.1.call-start = ((), (), s32[]{:S(2)}) async-start(), calls=%async_computation.18 | async-start | bytes 2097152 | tf_op jit(solution)/shard_map/psum | solution.py:124
  388.8 47.9 %copy-start.21 = (bf16[256,1024]{0,1:T(8,128)(2,1)}, bf16[256,1024]{0,1:T(8,128)(2,1)S(1)}, u32[]{:S(2)}) copy-start(bf16[256,1024]{0,1:T(8,128)(2,1)S(1)} %copy.66) | copy-start | bytes 1572868
  598.3 178.9 %all-gather.19.cloned.1.call-start = ((), (), s32[]{:S(2)}) async-start(), calls=%async_computation.14 | async-start | bytes 20971520 | tf_op jit(solution)/shard_map/all_gather | solution.py:254
  599.1 337.2 %all-gather.21.cloned.1.call-start = ((), (), s32[]{:S(2)}) async-start(), calls=%async_computation.15 | async-start | bytes 20971520 | tf_op jit(solution)/shard_map/all_gather | solution.py:256
  599.6 421.9 %all-reduce.22.cloned.1.call-start = ((), (), s32[]{:S(2)}) async-start(), calls=%async_computation.30 | async-start | bytes 4194304 | tf_op jit(solution)/shard_map/psum | solution.py:144
  608.0 421.0 %copy-start.56 = (f32[256]{0:T(256)}, f32[256]{0:T(256)S(1)}, u32[]{:S(2)}) copy-start(f32[256]{0:T(256)S(1)} %broadcast_multiply_fusion.2) | copy-start | bytes 3076
  619.0 410.0 %copy-start.63 = (f32[256]{0:T(256)}, f32[256]{0:T(256)S(1)}, u32[]{:S(2)}) copy-start(f32[256]{0:T(256)S(1)} %broadcast_multiply_fusion) | copy-start | bytes 3076
  619.6 409.5 %copy-start.68 = (f32[256]{0:T(256)}, f32[256]{0:T(256)S(1)}, u32[]{:S(2)}) copy-start(f32[256]{0:T(256)S(1)} %fusion.232) | copy-start | bytes 3076
  619.6 409.5 %copy-start.65 = (f32[256]{0:T(256)}, f32[256]{0:T(256)S(1)}, u32[]{:S(2)}) copy-start(f32[256]{0:T(256)S(1)} %fusion.230) | copy-start | bytes 3076
  1000.1 352.2 %reduce-scatter.16.cloned.1.call-start = ((), (), s32[]{:S(2)}) async-start(), calls=%async_computation.19 | async-start | bytes 5242880 | tf_op jit(solution)/shard_map/reduce_scatter | solution.py:165
  1161.2 185.8 %copy-start.25 = (bf16[16,256,64]{1,2,0:T(8,128)(2,1)}, bf16[16,256,64]{1,2,0:T(8,128)(2,1)S(1)}, u32[]{:S(2)}) copy-start(bf16[16,256,64]{1,2,0:T(8,128)(2,1)S(1)} %get-tuple-element.239) | copy-start | bytes 1572868
  1171.2 219.0 %reduce-scatter.18.cloned.1.call-start = ((), (), s32[]{:S(2)}) async-start(), calls=%async_computation.20 | async-start | bytes 5242880 | tf_op jit(solution)/shard_map/reduce_scatter | solution.py:165
  1302.1 47.6 %copy-start.23 = (bf16[16,256,64]{1,2,0:T(8,128)(2,1)}, bf16[16,256,64]{1,2,0:T(8,128)(2,1)S(1)}, u32[]{:S(2)}) copy-start(bf16[16,256,64]{1,2,0:T(8,128)(2,1)S(1)} %get-tuple-element.243) | copy-start | bytes 1572868
  1312.1 220.6 %all-reduce.20.cloned.1.call-start = ((), (), s32[]{:S(2)}) async-start(), calls=%async_computation.29 | async-start | bytes 8388608 | tf_op jit(solution)/shard_map/psum | solution.py:136
  1312.2 34.9 %slice-start = ((s8[12582912]{0:T(1024)(128)(4,1)}), s8[4194304]{0:T(1024)(128)(4,1)S(1)}, s32[]{:S(2)}) async-start(s8[12582912]{0:T(1024)(128)(4,1)} %bitcast.589), calls=%async_computation.31 | async-start | bytes 8388608
  1312.2 34.9 %slice-start.1 = ((s8[12582912]{0:T(1024)(128)(4,1)}), s8[4194304]{0:T(1024)(128)(4,1)S(1)}, s32[]{:S(2)}) async-start(s8[12582912]{0:T(1024)(128)(4,1)} %bitcast.589), calls=%async_computation.32 | async-start | bytes 8388608
  1399.1 141.0 %reduce-scatter.22.cloned.1.call-start = ((), (), s32[]{:S(2)}) async-start(), calls=%async_computation.22 | async-start | bytes 5242880 | tf_op jit(solution)/shard_map/reduce_scatter | solution.py:284
  1407.2 235.7 %reduce-scatter.24.cloned.1.call-start = ((), (), s32[]{:S(2)}) async-start(), calls=%async_computation.23 | async-start | bytes 20971520 | tf_op jit(solution)/shard_map/reduce_scatter | solution.py:290
  1446.2 353.7 %reduce-scatter.26.cloned.1.call-start = ((), (), s32[]{:S(2)}) async-start(), calls=%async_computation.24 | async-start | bytes 20971520 | tf_op jit(solution)/shard_map/reduce_scatter | solution.py:296
  1493.2 430.7 %reduce-scatter.20.cloned.1.call-start = ((), (), s32[]{:S(2)}) async-start(), calls=%async_computation.21 | async-start | bytes 15728640 | tf_op jit(solution)/shard_map/reduce_scatter | solution.py:278
  1528.4 423.3 %reduce-scatter.32.cloned.1.call-start = ((), (), s32[]{:S(2)}) async-start(), calls=%async_computation.27 | async-start | bytes 327680
  1532.5 447.1 %reduce-scatter.28.cloned.1.call-start = ((), (), s32[]{:S(2)}) async-start(), calls=%async_computation.25 | async-start | bytes 655360
  1538.9 469.2 %reduce-scatter.30.cloned.1.call-start = ((), (), s32[]{:S(2)}) async-start(), calls=%async_computation.26 | async-start | bytes 655360
  1540.1 899.0 %all-reduce.18.cloned.1.call-start = ((), (), s32[]{:S(2)}) async-start(), calls=%async_computation.28 | async-start | bytes 25165824 | tf_op jit(solution)/shard_map/psum | solution.py:306
  1923.9 28.7 %copy-start.10 = (bf16[256,2048]{1,0:T(8,128)(2,1)S(1)}, bf16[256,2048]{1,0:T(8,128)(2,1)}, u32[]{:S(2)}) copy-start(bf16[256,2048]{1,0:T(8,128)(2,1)} %all-reduce.16.cloned.1.call-done) | copy-start | bytes 3145732
  1923.9 28.7 %copy-start.81 = (f32[256]{0:T(256)S(1)}, f32[256]{0:T(256)}, u32[]{:S(2)}) copy-start(f32[256]{0:T(256)} %copy-done.80) | copy-start | bytes 3076
  1923.9 28.7 %copy-start.89 = (f32[256]{0:T(256)S(1)}, f32[256]{0:T(256)}, u32[]{:S(2)}) copy-start(f32[256]{0:T(256)} %copy-done.88) | copy-start | bytes 3076
  (87 other events, 499.6 us)
Sparse Core Ops, SparseCore 0:
  9.9 125.2 all-gather.10
  139.6 45.9 all-gather.12
  187.7 44.6 all-gather.14
  234.1 51.2 all-gather.16
  356.1 18.2 all-reduce.13
  380.7 47.1 all-gather.22
  430.1 44.6 all-gather.24
  598.4 18.3 all-reduce.15
  618.6 158.5 all-gather.18
  778.9 157.2 all-gather.20
  1000.2 21.2 all-reduce.21
  1171.3 77.9 reduce-scatter.15
  1312.2 77.9 reduce-scatter.17
  1399.3 29.2 all-reduce.19
  1431.9 53.8 reduce-scatter.21
  1489.0 153.7 reduce-scatter.23
  1646.1 153.7 reduce-scatter.25
  1803.1 120.7 reduce-scatter.19
  1927.5 24.0 reduce-scatter.31
  1954.8 24.7 reduce-scatter.27
  1983.2 24.7 reduce-scatter.29
  2011.0 428.0 all-reduce.17
where the time goes:
time: 2480 us; the launch traced here: 2460 us
  waiting for transfers between devices  1460 us (59%)
  matrix products  597 us (24%)
  local copies, waits for them, and re-layouts  157 us (6%)
  other arithmetic  152 us (6%)
  blocking collectives  77.3 us (3%)
    psum x1, waiting for transfers between devices, per_device(): lax.psum(shard_sums[2].astype(jnp.bfloat16), 'context').astype(jnp.float32)  414 us
    dot_general x76, matrix products, product(): return jnp.dot(left_op, right_op, preferred_element_type=jnp.float32)  190 us
    all_gather x1, waiting for transfers between devices, per_device(): lax.all_gather(w_up, 'fsdp', axis=0, tiled=True)  158 us
    reduce_scatter x1, waiting for transfers between devices, per_device(): lax.psum_scatter(totals[8].astype(jnp.bfloat16), 'fsdp', scatter_dimensio...  157 us
    dot_general x64, matrix products, masked_scores(): jnp.einsum('qd,kd->qk', queries, key_rows, preferred_element_type=jnp.flo...  150 us
    all_gather x1, waiting for transfers between devices, per_device(): lax.all_gather(w_down, 'fsdp', axis=1, tiled=True)  138 us
    reduce_scatter x1, waiting for transfers between devices, per_device(): lax.psum_scatter(totals[2].astype(jnp.bfloat16), 'fsdp', scatter_dimensio...  124 us
    all_gather x1, waiting for transfers between devices, per_device(): lax.all_gather(w_qkv, 'fsdp', axis=1, tiled=True)  109 us
  transfers between devices with their start and end apart: 22, of which 17 were waited for; matrix products, arithmetic and copies ran while one was open for 21% of the time, Pallas kernels for 0%

commit v1 on v0

--- a/solution.py
+++ b/solution.py
@@ -303,7 +303,9 @@
     reduced = (
         lax.psum(shard_sums[0].astype(jnp.bfloat16), "context").astype(jnp.float32),
         lax.psum(shard_sums[1].astype(jnp.bfloat16), "context").astype(jnp.float32),
-        lax.psum(shard_sums[2].astype(jnp.bfloat16), "context").astype(jnp.float32),
+        jnp.sum(lax.all_gather(shard_sums[2].astype(jnp.bfloat16), "context"), axis=0).astype(
+            jnp.float32
+        ),
         lax.psum(shard_sums[3].astype(jnp.bfloat16), "context").astype(jnp.float32),
         lax.psum(shard_sums[4].astype(jnp.bfloat16), "context").astype(jnp.float32),
         lax.psum(shard_sums[5].astype(jnp.bfloat16), "context").astype(jnp.float32),

time: 2480 us -> 2590 us (1.044)
  waiting for transfers between devices: 1460 us -> 1560 us
    all_gather x0 -> x1, waiting for transfers between devices: none -> 203 us  [per_device(): lax.all_gather(shard_sums[2].astype(jnp.bfloat16), 'context')]
    psum x1, waiting for transfers between devices: 414 us -> 312 us  [per_device(): lax.psum(shard_sums[4].astype(jnp.bfloat16), 'context').astype(jnp.float32)]
  transfers between devices with their start and end apart: 22 -> 23, of which waited for: 17 -> 19; matrix products, arithmetic and copies ran while one was open for 21% -> 21% of each run, Pallas kernels for 0% -> 0%
where the time goes in v1:
time: 2590 us; the launch traced here: 2570 us
  waiting for transfers between devices  1560 us (60%)
  matrix products  597 us (23%)
  other arithmetic  163 us (6%)
  local copies, waits for them, and re-layouts  157 us (6%)
  blocking collectives  77.4 us (3%)
    psum x1, waiting for transfers between devices, per_device(): lax.psum(shard_sums[4].astype(jnp.bfloat16), 'context').astype(jnp.float32)  312 us
    all_gather x1, waiting for transfers between devices, per_device(): lax.all_gather(shard_sums[2].astype(jnp.bfloat16), 'context')  203 us
    dot_general x76, matrix products, product(): return jnp.dot(left_op, right_op, preferred_element_type=jnp.float32)  190 us
    all_gather x1, waiting for transfers between devices, per_device(): lax.all_gather(w_up, 'fsdp', axis=0, tiled=True)  158 us
    reduce_scatter x1, waiting for transfers between devices, per_device(): lax.psum_scatter(totals[8].astype(jnp.bfloat16), 'fsdp', scatter_dimensio...  157 us
    dot_general x64, matrix products, masked_scores(): jnp.einsum('qd,kd->qk', queries, key_rows, preferred_element_type=jnp.flo...  150 us
    all_gather x1, waiting for transfers between devices, per_device(): lax.all_gather(w_down, 'fsdp', axis=1, tiled=True)  138 us
    reduce_scatter x1, waiting for transfers between devices, per_device(): lax.psum_scatter(totals[2].astype(jnp.bfloat16), 'fsdp', scatter_dimensio...  124 us
  transfers between devices with their start and end apart: 23, of which 19 were waited for; matrix products, arithmetic and copies ran while one was open for 21% of the time, Pallas kernels for 0%

profile of v1, /device:TPU:0, one launch (start us, length us, event | category | flops | bytes accessed | tf_op | source)
XLA Modules:
  0.0 2574.8 jit_solution(5540722415649833067)
XLA Ops:
  8.0 9.6 all_gather.59
  17.6 7.9 all_gather.58
  26.4 108.7 %all-gather.13.cloned.1.call-done = bf16[3,2048,1024]{2,1,0:T(8,128)(2,1)} async-done(((bf16[3,512,1024]{2,1,0:T(8,128)(2,1)}), bf16[3,2048,1024]{2,1,0:T(8,128)(2,1)}) %all-gather.13.cloned.1.call-update) | async-done | bytes 12582928 | tf_op jit(solution)/shard_map/all_gather | solution.py:250
  139.5 8.0 all_gather.61
  160.1 25.4 all-gather.15.cloned.1.call-done
  194.2 38.1 %all-gather.17.cloned.1.call-done = bf16[1024,1024]{1,0:T(8,128)(2,1)} async-done(((bf16[256,1024]{1,0:T(8,128)(2,1)}), bf16[1024,1024]{1,0:T(8,128)(2,1)}) %all-gather.17.cloned.1.call-update) | async-done | bytes 2097168 | tf_op jit(solution)/shard_map/all_gather | solution.py:108
  236.3 4.9 copy.65
  246.6 104.7 %while.60 = (s32[]{:T(128)}, bf16[16,256,64]{1,2,0:T(8,128)(2,1)}, f32[16,256]{1,0:T(8,128)S(1)}, bf16[16,256,1024]{2,1,0:T(8,128)(2,1)}, bf16[16,256,64]{2,1,0:...) while((s32[]{:T(128)}, bf16[16,256,64]{1,2,0:T(8,128)(2,1)}, ...), condition=%wide.region_5.6_spmd.clone.clone, body=%wide.region_2.5_spmd.clone.clone.sunk | while | flops 71565056 | bytes 5920409 | solution.py:119
  356.0 8.2 all-gather.1
  364.2 10.1 all-reduce.14.cloned.1.call-done
  390.1 37.8 %all-gather.25.cloned.1.call-done = bf16[1024,1024]{1,0:T(8,128)(2,1)} async-done(((bf16[256,1024]{1,0:T(8,128)(2,1)}), bf16[1024,1024]{1,0:T(8,128)(2,1)}) %all-gather.25.cloned.1.call-update) | async-done | bytes 2097168 | tf_op jit(solution)/shard_map/all_gather | solution.py:107
  436.7 38.1 %all-gather.27.cloned.1.call-done = bf16[1024,1024]{1,0:T(8,128)(2,1)} async-done(((bf16[256,1024]{1,0:T(8,128)(2,1)}), bf16[1024,1024]{1,0:T(8,128)(2,1)}) %all-gather.27.cloned.1.call-update) | async-done | bytes 2097168 | tf_op jit(solution)/shard_map/all_gather | solution.py:108
  488.9 104.7 %while.61 = (s32[]{:T(128)}, bf16[16,256,64]{1,2,0:T(8,128)(2,1)}, f32[16,256]{1,0:T(8,128)S(1)}, bf16[16,256,1024]{2,1,0:T(8,128)(2,1)}, bf16[16,256,64]{2,1,0:...) while((s32[]{:T(128)}, bf16[16,256,64]{1,2,0:T(8,128)(2,1)}, ...), condition=%wide.region_15.16_spmd.clone.clone, body=%wide.region_12.15_spmd.clone.clone.sunk | while | flops 71565056 | bytes 5920409 | solution.py:119
  599.7 8.2 all_gather.67
  608.0 8.8 all-reduce.16.cloned.1.call-done
  619.6 157.6 %all-gather.21.cloned.1.call-done = bf16[2048,4096]{1,0:T(8,128)(2,1)} async-done(((bf16[512,4096]{1,0:T(8,128)(2,1)}), bf16[2048,4096]{1,0:T(8,128)(2,1)}) %all-gather.21.cloned.1.call-update) | async-done | bytes 16777232 | tf_op jit(solution)/shard_map/all_gather | solution.py:254
  777.2 13.2 convolution_add_fusion
  791.6 6.3 convolution_add_fusion.1
  797.9 138.3 %all-gather.23.cloned.1.call-done = bf16[4096,2048]{1,0:T(8,128)(2,1)} async-done(((bf16[4096,512]{1,0:T(8,128)(2,1)}), bf16[4096,2048]{1,0:T(8,128)(2,1)}) %all-gather.23.cloned.1.call-update) | async-done | bytes 16777232 | tf_op jit(solution)/shard_map/all_gather | solution.py:256
  936.2 20.2 convert_reduce_fusion.1
  956.4 11.9 convolution_convert_fusion.1
  968.3 19.9 convert_reduce_fusion
  988.2 11.9 convolution_convert_fusion
  1000.2 21.4 all-reduce.22.cloned.1.call-done
  1040.2 121.2 %while.62 = (s32[]{:T(128)}, bf16[16,256,64]{1,2,0:T(8,128)(2,1)S(1)}, bf16[16,256,1024]{2,1,0:T(8,128)(2,1)}, bf16[16,256,64]{2,1,0:T(8,128)(2,1)}, bf16[16,102...) while((s32[]{:T(128)}, ...), condition=%wide.region_25.26_spmd.clone.clone, body=%wide.region_23.25_spmd.clone.clone.sunk | while | flops 104349440 | bytes 8306329 | solution.py:154
  1161.4 5.2 convolution_convert_fusion.7
  1181.0 121.3 %while.63 = (s32[]{:T(128)}, bf16[16,256,64]{1,2,0:T(8,128)(2,1)S(1)}, bf16[16,256,1024]{2,1,0:T(8,128)(2,1)}, bf16[16,256,64]{2,1,0:T(8,128)(2,1)}, bf16[16,102...) while((s32[]{:T(128)}, ...), condition=%wide.region_35.36_spmd.clone.clone, body=%wide.region_33.35_spmd.clone.clone.sunk | while | flops 104349440 | bytes 8306329 | solution.py:154
  1302.3 5.2 convolution_convert_fusion.6
  1312.3 17.7 convolution_convert_fusion.2
  1330.0 17.1 convolution_convert_fusion.3
  1361.4 28.9 %reduce-scatter.18.cloned.1.call-done = bf16[256,2,1024]{0,2,1:T(8,128)(2,1)} async-done(((bf16[1024,2,1024]{0,2,1:T(8,128)(2,1)}), bf16[256,2,1024]{0,2,1:T(8,128)(2,1)}) %reduce-scatter.18.cloned.1.call-update) | async-done | bytes 1048592 | tf_op jit(solution)/shard_map/reduce_scatter | solution.py:165
  1409.9 17.0 fusion.233
  1426.9 19.4 add_convert_fusion.1
  1446.4 21.1 fusion.176
  1467.5 25.8 %add_convert_fusion = bf16[4096,2048]{1,0:T(8,128)(2,1)} fusion(f32[4096,2048]{1,0:T(8,128)} %fusion.176, bf16[2,256,2048]{2,1,0:T(8,128)(2,1)} %param.23, f32[256,4096]{1,0:T(8,128)} %convolution_add_fusion), kind=kOutput, calls=%fused_computation.104 | convolution fusion | flops 4379901952 | bytes 55574528 | tf_op jit(solution)/shard_map/dot_general | solution.py:21
  1513.0 15.5 fusion.80
  1540.3 102.7 %reduce-scatter.24.cloned.1.call-done = bf16[512,4096]{1,0:T(8,128)(2,1)} async-done(((bf16[2048,4096]{1,0:T(8,128)(2,1)}), bf16[512,4096]{1,0:T(8,128)(2,1)}) %reduce-scatter.24.cloned.1.call-update) | async-done | bytes 4194320 | tf_op jit(solution)/shard_map/reduce_scatter | solution.py:290
  1643.0 157.0 %reduce-scatter.26.cloned.1.call-done = bf16[4096,512]{1,0:T(8,128)(2,1)} async-done(((bf16[4096,2048]{1,0:T(8,128)(2,1)}), bf16[4096,512]{1,0:T(8,128)(2,1)}) %reduce-scatter.26.cloned.1.call-update) | async-done | bytes 4194320 | tf_op jit(solution)/shard_map/reduce_scatter | solution.py:296
  1800.2 123.9 %reduce-scatter.20.cloned.1.call-done = bf16[3,512,1024]{2,1,0:T(8,128)(2,1)} async-done(((bf16[3,2048,1024]{2,1,0:T(8,128)(2,1)}), bf16[3,512,1024]{2,1,0:T(8,128)(2,1)}) %reduce-scatter.20.cloned.1.call-update) | async-done | bytes 3145744 | tf_op jit(solution)/shard_map/reduce_scatter | solution.py:278
  1924.1 7.9 all-gather.2
  1935.9 15.1 all-reduce.5
  1962.4 17.4 reduce-scatter.28.cloned.1.call-done
  1980.8 27.5 %reduce-scatter.30.cloned.1.call-done = bf16[512,2]{1,0:T(8,128)(2,1)} async-done(((bf16[2048,2]{1,0:T(8,128)(2,1)}), bf16[512,2]{1,0:T(8,128)(2,1)}) %reduce-scatter.30.cloned.1.call-update) | async-done | bytes 2064
  2009.2 12.5 all-reduce.3
  2025.3 312.0 %all-reduce.18.cloned.1.call-done = (bf16[1024,512]{1,0:T(8,128)(2,1)}, bf16[512,4096]{1,0:T(8,128)(2,1)}, bf16[4096,512]{1,0:T(8,128)(2,1)}) async-done(((bf16[1024,512]{1,0:T(8,128)(2,1)}, bf16[512,4096]{1,0:T(8,128)(2,1)}, bf16[4096,512]{1,0:T(8,128)(2,1)}), (bf16[1024,512]{1,0:T(8,128)(2,1)}, bf16[512,4096]{1,0:T(8,128)(2,1)}, bf16[4096,512]{1,0:T(8,128)(2,1)})) %all-reduce.18.cloned.1.call-update) | async-done | bytes 9437200 | tf_op jit(solution)/shard_map/psum | solution.py:310
  2340.0 7.7 convert_element_type.485
  2352.5 203.4 %all-gather.29.cloned.1.call-done = bf16[12,512,1024]{2,1,0:T(8,128)(2,1)} async-done(((bf16[3,512,1024]{2,1,0:T(8,128)(2,1)}), bf16[12,512,1024]{2,1,0:T(8,128)(2,1)}) %all-gather.29.cloned.1.call-update) | async-done | bytes 12582928 | tf_op jit(solution)/shard_map/all_gather | solution.py:306
  2555.9 8.7 reduce_sum.442
  (895 shorter events, 673.1 us)
Async XLA Ops:
  7.2 127.9 %all-gather.13.cloned.1.call-start = ((), (), s32[]{:S(2)}) async-start(), calls=%async_computation.9 | async-start | bytes 15728640 | tf_op jit(solution)/shard_map/all_gather | solution.py:250
  7.9 177.6 %all-gather.15.cloned.1.call-start = ((), (), s32[]{:S(2)}) async-start(), calls=%async_computation.10 | async-start | bytes 2621440 | tf_op jit(solution)/shard_map/all_gather | solution.py:107
  25.9 129.2 %copy-start.52 = (f32[256]{0:T(256)}, f32[256]{0:T(256)S(1)}, u32[]{:S(2)}) copy-start(f32[256]{0:T(256)S(1)} %broadcast_multiply_fusion.3) | copy-start | bytes 3076
  26.3 113.1 %copy-start.88 = (f32[256]{0:T(256)}, f32[256]{0:T(256)S(1)}, u32[]{:S(2)}) copy-start(f32[256]{0:T(256)S(1)} %fusion.133) | copy-start | bytes 3076
  26.3 128.7 %copy-start.57 = (f32[256]{0:T(256)}, f32[256]{0:T(256)S(1)}, u32[]{:S(2)}) copy-start(f32[256]{0:T(256)S(1)} %fusion.229) | copy-start | bytes 3076
  26.4 358.7 %copy-start.41 = (f32[1,2048]{1,0:T(1,128)}, f32[1,2048]{1,0:T(1,128)S(1)}, u32[]{:S(2)}) copy-start(f32[1,2048]{1,0:T(1,128)S(1)} %get-tuple-element.761) | copy-start | bytes 24580
  26.4 764.1 %copy-start.48 = (f32[1,2048]{1,0:T(1,128)}, f32[1,2048]{1,0:T(1,128)S(1)}, u32[]{:S(2)}) copy-start(f32[1,2048]{1,0:T(1,128)S(1)} %get-tuple-element.760) | copy-start | bytes 24580
  26.4 358.6 %copy-start.27 = (f32[1,2048]{1,0:T(1,128)}, f32[1,2048]{1,0:T(1,128)S(1)}, u32[]{:S(2)}) copy-start(f32[1,2048]{1,0:T(1,128)S(1)} %get-tuple-element.759) | copy-start | bytes 24580
  26.4 1002.6 %copy-start.46 = (f32[1,2048]{1,0:T(1,128)}, f32[1,2048]{1,0:T(1,128)S(1)}, u32[]{:S(2)}) copy-start(f32[1,2048]{1,0:T(1,128)S(1)} %get-tuple-element.758) | copy-start | bytes 24580
  139.4 92.9 %all-gather.17.cloned.1.call-start = ((), (), s32[]{:S(2)}) async-start(), calls=%async_computation.11 | async-start | bytes 2621440 | tf_op jit(solution)/shard_map/all_gather | solution.py:108
  152.0 199.3 %all-gather.19.cloned.1.call-start = ((), (), s32[]{:S(2)}) async-start(), calls=%async_computation.12 | async-start | bytes 5242880 | tf_op jit(solution)/shard_map/all_gather | solution.py:252
  152.6 221.7 %all-reduce.14.cloned.1.call-start = ((), (), s32[]{:S(2)}) async-start(), calls=%async_computation.13 | async-start | bytes 2097152 | tf_op jit(solution)/shard_map/psum | solution.py:124
  158.8 35.4 %copy-start.19 = (bf16[256,1024]{0,1:T(8,128)(2,1)}, bf16[256,1024]{0,1:T(8,128)(2,1)S(1)}, u32[]{:S(2)}) copy-start(bf16[256,1024]{0,1:T(8,128)(2,1)S(1)} %copy.60) | copy-start | bytes 1572868
  356.0 71.9 %all-gather.25.cloned.1.call-start = ((), (), s32[]{:S(2)}) async-start(), calls=%async_computation.16 | async-start | bytes 2621440 | tf_op jit(solution)/shard_map/all_gather | solution.py:107
  364.2 664.8 %copy-start.43 = (f32[4,1,512]{2,1,0:T(1,128)}, f32[4,1,512]{2,1,0:T(1,128)S(1)}, u32[]{:S(2)}) copy-start(f32[4,1,512]{2,1,0:T(1,128)S(1)} %convert_element_type.494) | copy-start | bytes 24580
  380.6 94.2 %all-gather.27.cloned.1.call-start = ((), (), s32[]{:S(2)}) async-start(), calls=%async_computation.17 | async-start | bytes 2621440 | tf_op jit(solution)/shard_map/all_gather | solution.py:108
  385.0 231.8 %all-reduce.16.cloned.1.call-start = ((), (), s32[]{:S(2)}) async-start(), calls=%async_computation.18 | async-start | bytes 2097152 | tf_op jit(solution)/shard_map/psum | solution.py:124
  388.8 47.9 %copy-start.21 = (bf16[256,1024]{0,1:T(8,128)(2,1)}, bf16[256,1024]{0,1:T(8,128)(2,1)S(1)}, u32[]{:S(2)}) copy-start(bf16[256,1024]{0,1:T(8,128)(2,1)S(1)} %copy.66) | copy-start | bytes 1572868
  598.3 178.9 %all-gather.21.cloned.1.call-start = ((), (), s32[]{:S(2)}) async-start(), calls=%async_computation.14 | async-start | bytes 20971520 | tf_op jit(solution)/shard_map/all_gather | solution.py:254
  599.1 337.1 %all-gather.23.cloned.1.call-start = ((), (), s32[]{:S(2)}) async-start(), calls=%async_computation.15 | async-start | bytes 20971520 | tf_op jit(solution)/shard_map/all_gather | solution.py:256
  599.6 421.9 %all-reduce.22.cloned.1.call-start = ((), (), s32[]{:S(2)}) async-start(), calls=%async_computation.31 | async-start | bytes 4194304 | tf_op jit(solution)/shard_map/psum | solution.py:144
  608.0 421.1 %copy-start.54 = (f32[256]{0:T(256)}, f32[256]{0:T(256)S(1)}, u32[]{:S(2)}) copy-start(f32[256]{0:T(256)S(1)} %broadcast_multiply_fusion.2) | copy-start | bytes 3076
  619.0 410.1 %copy-start.61 = (f32[256]{0:T(256)}, f32[256]{0:T(256)S(1)}, u32[]{:S(2)}) copy-start(f32[256]{0:T(256)S(1)} %broadcast_multiply_fusion) | copy-start | bytes 3076
  619.6 409.5 %copy-start.66 = (f32[256]{0:T(256)}, f32[256]{0:T(256)S(1)}, u32[]{:S(2)}) copy-start(f32[256]{0:T(256)S(1)} %fusion.232) | copy-start | bytes 3076
  619.6 409.5 %copy-start.63 = (f32[256]{0:T(256)}, f32[256]{0:T(256)S(1)}, u32[]{:S(2)}) copy-start(f32[256]{0:T(256)S(1)} %fusion.230) | copy-start | bytes 3076
  1000.1 352.3 %reduce-scatter.16.cloned.1.call-start = ((), (), s32[]{:S(2)}) async-start(), calls=%async_computation.19 | async-start | bytes 5242880 | tf_op jit(solution)/shard_map/reduce_scatter | solution.py:165
  1161.4 185.8 %copy-start.25 = (bf16[16,256,64]{1,2,0:T(8,128)(2,1)}, bf16[16,256,64]{1,2,0:T(8,128)(2,1)S(1)}, u32[]{:S(2)}) copy-start(bf16[16,256,64]{1,2,0:T(8,128)(2,1)S(1)} %get-tuple-element.239) | copy-start | bytes 1572868
  1171.3 219.0 %reduce-scatter.18.cloned.1.call-start = ((), (), s32[]{:S(2)}) async-start(), calls=%async_computation.20 | async-start | bytes 5242880 | tf_op jit(solution)/shard_map/reduce_scatter | solution.py:165
  1302.2 47.6 %copy-start.23 = (bf16[16,256,64]{1,2,0:T(8,128)(2,1)}, bf16[16,256,64]{1,2,0:T(8,128)(2,1)S(1)}, u32[]{:S(2)}) copy-start(bf16[16,256,64]{1,2,0:T(8,128)(2,1)S(1)} %get-tuple-element.243) | copy-start | bytes 1572868
  1312.2 220.6 %all-reduce.20.cloned.1.call-start = ((), (), s32[]{:S(2)}) async-start(), calls=%async_computation.30 | async-start | bytes 8388608 | tf_op jit(solution)/shard_map/psum | solution.py:136
  1399.3 141.0 %reduce-scatter.22.cloned.1.call-start = ((), (), s32[]{:S(2)}) async-start(), calls=%async_computation.22 | async-start | bytes 5242880 | tf_op jit(solution)/shard_map/reduce_scatter | solution.py:284
  1407.3 235.7 %reduce-scatter.24.cloned.1.call-start = ((), (), s32[]{:S(2)}) async-start(), calls=%async_computation.23 | async-start | bytes 20971520 | tf_op jit(solution)/shard_map/reduce_scatter | solution.py:290
  1446.4 353.7 %reduce-scatter.26.cloned.1.call-start = ((), (), s32[]{:S(2)}) async-start(), calls=%async_computation.24 | async-start | bytes 20971520 | tf_op jit(solution)/shard_map/reduce_scatter | solution.py:296
  1493.3 430.7 %reduce-scatter.20.cloned.1.call-start = ((), (), s32[]{:S(2)}) async-start(), calls=%async_computation.21 | async-start | bytes 15728640 | tf_op jit(solution)/shard_map/reduce_scatter | solution.py:278
  1528.5 423.2 %reduce-scatter.32.cloned.1.call-start = ((), (), s32[]{:S(2)}) async-start(), calls=%async_computation.28 | async-start | bytes 327680
  1532.6 447.1 %reduce-scatter.28.cloned.1.call-start = ((), (), s32[]{:S(2)}) async-start(), calls=%async_computation.26 | async-start | bytes 655360
  1539.0 469.2 %reduce-scatter.30.cloned.1.call-start = ((), (), s32[]{:S(2)}) async-start(), calls=%async_computation.27 | async-start | bytes 655360
  1540.2 797.0 %all-reduce.18.cloned.1.call-start = ((), (), s32[]{:S(2)}) async-start(), calls=%async_computation.29 | async-start | bytes 18874368 | tf_op jit(solution)/shard_map/psum | solution.py:310
  1800.0 124.1 %copy-start.98 = (bf16[512]{0:T(512)(128)(2,1)S(1)}, bf16[512]{0:T(512)(128)(2,1)}, u32[]{:S(2)}) copy-start(bf16[512]{0:T(512)(128)(2,1)} %param.35) | copy-start | bytes 3076
  1800.0 132.0 %copy-start.106 = (u32[32]{0:T(128)S(1)}, u32[32]{0:T(128)}, u32[]{:S(2)}) copy-start(u32[32]{0:T(128)} %constant.209) | copy-start | bytes 388
  1800.0 135.8 %copy-start.80 = (f32[4096]{0:T(1024)S(1)}, f32[4096]{0:T(1024)}, u32[]{:S(2)}) copy-start(f32[4096]{0:T(1024)} %get-tuple-element.768) | copy-start | bytes 49156
  1800.1 135.8 %copy-start.81 = (f32[4096]{0:T(1024)S(1)}, f32[4096]{0:T(1024)}, u32[]{:S(2)}) copy-start(f32[4096]{0:T(1024)} %get-tuple-element.770) | copy-start | bytes 49156
  1800.1 135.8 %copy-start.72 = (f32[2048]{0:T(1024)S(1)}, f32[2048]{0:T(1024)}, u32[]{:S(2)}) copy-start(f32[2048]{0:T(1024)} %get-tuple-element.740) | copy-start | bytes 24580
  1800.1 135.8 %copy-start.73 = (f32[2048]{0:T(1024)S(1)}, f32[2048]{0:T(1024)}, u32[]{:S(2)}) copy-start(f32[2048]{0:T(1024)} %get-tuple-element.752) | copy-start | bytes 24580
  1800.1 152.6 %copy-start.10 = (bf16[256,2048]{1,0:T(8,128)(2,1)S(1)}, bf16[256,2048]{1,0:T(8,128)(2,1)}, u32[]{:S(2)}) copy-start(bf16[256,2048]{1,0:T(8,128)(2,1)} %all-reduce.16.cloned.1.call-done) | copy-start | bytes 3145732
  1800.1 152.6 %copy-start.79 = (f32[256]{0:T(256)S(1)}, f32[256]{0:T(256)}, u32[]{:S(2)}) copy-start(f32[256]{0:T(256)} %copy-done.78) | copy-start | bytes 3076
  1800.1 152.6 %copy-start.87 = (f32[256]{0:T(256)S(1)}, f32[256]{0:T(256)}, u32[]{:S(2)}) copy-start(f32[256]{0:T(256)} %copy-done.86) | copy-start | bytes 3076
  1800.1 755.8 %all-gather.29.cloned.1.call-start = ((), (), s32[]{:S(2)}) async-start(), calls=%async_computation.25 | async-start | bytes 15728640 | tf_op jit(solution)/shard_map/all_gather | solution.py:306
  (86 other events, 621.6 us)
Sparse Core Ops, SparseCore 0:
  9.9 125.2 all-gather.12
  139.6 45.9 all-gather.14
  187.7 44.6 all-gather.16
  234.1 51.2 all-gather.18
  356.1 18.2 all-reduce.13
  380.7 47.1 all-gather.24
  430.1 44.6 all-gather.26
  598.4 18.2 all-reduce.15
  618.6 158.5 all-gather.20
  778.9 157.2 all-gather.22
  1000.2 21.2 all-reduce.21
  1171.5 77.9 reduce-scatter.15
  1312.4 77.9 reduce-scatter.17
  1399.4 29.2 all-reduce.19
  1432.1 53.8 reduce-scatter.21
  1489.2 153.7 reduce-scatter.23
  1646.2 153.7 reduce-scatter.25
  1803.3 120.7 reduce-scatter.19
  1927.6 24.0 reduce-scatter.31
  1955.0 24.7 reduce-scatter.27
  1983.4 24.7 reduce-scatter.29
  2011.1 326.0 all-reduce.17
  2338.8 217.0 all-gather.28
